TPU v7x, 32 devices: a whole 2x2x4 slice. The times are simulated.
32 devices in a mesh: ctx: 8 (over y, x, core), ch: 4 (over z).
Axes of the slice: x: 2, y: 2, z: 4, core: 2. Of those that a mesh axis runs over, the one named last changes fastest.
Arguments:
- query_act: bfloat16 [2048, 8192], P('ctx', 'ch'), may hold values from -6 to 6
- key_act: bfloat16 [2048, 8192], P('ctx', 'ch'), may hold values from -6 to 6
- value_act: bfloat16 [2048, 8192], P('ctx', 'ch'), may hold values from -6 to 6
- out_grad: bfloat16 [2048, 8192], P('ctx', 'ch'), may hold values from -6 to 6
- out_weight: bfloat16 [8192, 8192], P('ctx', 'ch'), may hold values from -0.0625 to 0.0625
- token_mask: int32 [2048], P('ctx'), may hold values from 0 to 1, as said below
- decay_rate: float32 [16, 8192], P(None, 'ch'), may hold values from 4.8828125e-05 to 0.033
- residue: float32 [16, 8192], P(None, 'ch'), may hold values from -75 to 75
Outputs:
- query_grad: bfloat16 [2048, 8192], P('ctx', 'ch')
- key_grad: bfloat16 [2048, 8192], P('ctx', 'ch')
- value_grad: bfloat16 [2048, 8192], P('ctx', 'ch')
- filter_grad: float32 [16, 8192], P(None, 'ch')
Inputs may be any that keep to these rules, and one draw needn't show every extreme that they name: `token_mask`: 1 marks a valid token; within each aligned run of 64 positions the valid tokens come first.
All inputs are finite; a program needn't handle non-finite values.
Results may differ from a plain program's by a relative error of at most 0.0015.
Values may be sent and summed in bfloat16 or wider, within the bound.
A program may use at most 192 MiB of HBM per device.

v0:
```python
import jax
import jax.numpy as jnp
from jax import lax
from jax.sharding import PartitionSpec as P


def carried_in(shard, axis, combine, identity, reverse):
    devices, here = (lax.axis_size(axis), lax.axis_index(axis))
    everything = jax.tree.map(lambda part: lax.all_gather(part, axis), shard)
    start = jax.tree.map(
        lambda part, zero: jnp.broadcast_to(jnp.asarray(zero, part.dtype), part.shape),
        shard,
        identity,
    )

    def turn(k, before):
        at = devices - 1 - k if reverse else k
        reached = at > here if reverse else at < here
        new = combine(before, jax.tree.map(lambda part: part[at], everything))
        return jax.tree.map(lambda a, b: jnp.where(reached, a, b), new, before)

    return lax.fori_loop(0, devices, turn, start)


def chain_join(earlier, later):
    return (earlier[0] * later[0], later[0] * earlier[1] + later[1])


def body(query_act, key_act, value_act, out_grad, out_weight, token_mask, decay_rate, residue):
    rows_block = 64
    tokens_here = query_act.shape[0]
    chans = query_act.shape[1]
    modes = decay_rate.shape[0]
    blocks = tokens_here // rows_block
    live = token_mask.astype(jnp.float32)[:, None]
    inputs = live * key_act.astype(jnp.float32) * value_act.astype(jnp.float32)
    root_gain = jnp.sqrt(-jnp.expm1(-2.0 * decay_rate))
    filter_gain = residue * root_gain
    places = jnp.arange(rows_block).astype(jnp.float32)[:, None, None]
    rising = jnp.exp(decay_rate[None] * places)
    falling = jnp.exp(-decay_rate[None] * places)
    step_decay = jnp.exp(-decay_rate)
    trailing = jnp.exp(-decay_rate[None] * (rows_block - places))
    row_ids = lax.broadcasted_iota(jnp.int32, (rows_block, rows_block), 0)
    col_ids = lax.broadcasted_iota(jnp.int32, (rows_block, rows_block), 1)
    lower_ones = (row_ids >= col_ids).astype(jnp.float32)
    upper_ones = (row_ids <= col_ids).astype(jnp.float32)
    zeros = jnp.zeros((modes, chans), jnp.float32)

    def forward_block(carried, block_in):
        scaled = (rising * block_in[:, None, :]).reshape(rows_block, modes * chans)
        summed = jnp.dot(lower_ones, scaled, precision=lax.Precision.HIGHEST).reshape(
            rows_block, modes, chans
        )
        states = falling * summed + falling * step_decay[None] * carried[None]
        return (states[-1], jnp.sum(filter_gain[None] * states, axis=1))

    end_state, conv_local = lax.scan(
        forward_block, zeros, inputs.reshape(blocks, rows_block, chans)
    )
    conv_local = conv_local.reshape(tokens_here, chans)
    full_grad = lax.all_gather(out_grad, "ch", axis=1, tiled=True)
    gate_grad = jnp.dot(
        full_grad,
        lax.all_gather(out_weight, "ctx", axis=0, tiled=True),
        preferred_element_type=jnp.float32,
    )
    conv_grad = gate_grad * query_act.astype(jnp.float32)

    def backward_block(carry, block_in):
        carried, running = carry
        grad_blk, input_blk = block_in
        scaled = (falling * grad_blk[:, None, :]).reshape(rows_block, modes * chans)
        summed = jnp.dot(upper_ones, scaled, precision=lax.Precision.HIGHEST).reshape(
            rows_block, modes, chans
        )
        states = rising * summed + trailing * carried[None]
        running = running + jnp.sum(input_blk[:, None, :] * states, axis=0)
        return ((states[0], running), jnp.sum(filter_gain[None] * states, axis=1))

    (start_state, filter_local), grad_local = lax.scan(
        backward_block,
        (zeros, zeros),
        (conv_grad.reshape(blocks, rows_block, chans), inputs.reshape(blocks, rows_block, chans)),
        reverse=True,
    )
    grad_local = grad_local.reshape(tokens_here, chans)
    span_decay = jnp.exp(-decay_rate * tokens_here)
    forward_in = carried_in(
        (span_decay, end_state), "ctx", chain_join, (jnp.ones_like(span_decay), zeros), False
    )[1]
    backward_in = carried_in(
        (span_decay, start_state), "ctx", chain_join, (jnp.ones_like(span_decay), zeros), True
    )[1]
    token_places = jnp.arange(tokens_here).astype(jnp.float32)[:, None, None]
    conv = conv_local + jnp.sum(
        jnp.exp(-decay_rate[None] * (token_places + 1.0)) * (filter_gain * forward_in)[None], axis=1
    )
    input_grad = grad_local + jnp.sum(
        jnp.exp(-decay_rate[None] * (tokens_here - token_places))
        * (filter_gain * backward_in)[None],
        axis=1,
    )
    query_grad = (gate_grad * conv).astype(jnp.bfloat16)
    key_grad = (live * input_grad * value_act.astype(jnp.float32)).astype(jnp.bfloat16)
    value_grad = (live * input_grad * key_act.astype(jnp.float32)).astype(jnp.bfloat16)
    filter_terms = root_gain * (filter_local + backward_in * step_decay * end_state)
    filter_grad = lax.psum(filter_terms, "ctx")
    return (query_grad, key_grad, value_grad, filter_grad)


def solution(mesh):
    placed = (
        P("ctx", "ch"),
        P("ctx", "ch"),
        P("ctx", "ch"),
        P("ctx", "ch"),
        P("ctx", "ch"),
        P("ctx"),
        P(None, "ch"),
        P(None, "ch"),
    )
    return jax.shard_map(
        body,
        mesh=mesh,
        in_specs=placed,
        out_specs=(P("ctx", "ch"), P("ctx", "ch"), P("ctx", "ch"), P(None, "ch")),
        check_vma=False,
    )
```

profile of v0, /device:TPU:0, one launch (start us, length us, event | category | flops | bytes accessed | tf_op | source)
XLA Modules:
  0.0 719.4 jit_solution(11028100770254350850)
XLA Ops:
  14.7 100.9 %while.67 = (s32[]{:T(128)}, f32[16,2048]{1,0:T(8,128)S(1)}, f32[4,64,2048]{2,1,0:T(8,128)}, f32[4,64,2048]{2,1,0:T(8,128)S(1)}, f32[16,2048]{1,0:T(8,128)S(1)},...) while((s32[]{:T(128)}, f32[16,2048]{1,0:T(8,128)S(1)}, ...), condition=%wide.region_2.3_spmd.clone.clone, body=%wide.region_0.2_spmd.clone.clone.sunk | while | flops 1629364224 | bytes 79561336 | solution.py:58
  21.2 8.5 %fusion.52 = f32[32768,64]{0,1:T(8,128)S(1)} fusion(f32[64,32768]{1,0:T(8,128)S(1)} %bitcast.141), kind=kOutput, calls=%fused_computation.23.clone.1 | convolution fusion | flops 1610620928 | bytes 16777216 | tf_op jit(solution)/shard_map/while/body/eval_jaxpr/dot_general | solution.py:52
  71.5 8.5 %fusion.52 = f32[32768,64]{0,1:T(8,128)S(1)} fusion(f32[64,32768]{1,0:T(8,128)S(1)} %bitcast.141), kind=kOutput, calls=%fused_computation.23.clone.1 | convolution fusion | flops 1610620928 | bytes 16777216 | tf_op jit(solution)/shard_map/while/body/eval_jaxpr/dot_general | solution.py:52
  96.6 8.5 %fusion.52 = f32[32768,64]{0,1:T(8,128)S(1)} fusion(f32[64,32768]{1,0:T(8,128)S(1)} %bitcast.141), kind=kOutput, calls=%fused_computation.23.clone.1 | convolution fusion | flops 1610620928 | bytes 16777216 | tf_op jit(solution)/shard_map/while/body/eval_jaxpr/dot_general | solution.py:52
  117.6 136.5 %all-gather.11.cloned.1.call-done = bf16[8192,2048]{1,0:T(8,128)(2,1)} async-done(((bf16[1024,2048]{1,0:T(8,128)(2,1)}), bf16[8192,2048]{1,0:T(8,128)(2,1)}) %all-gather.11.cloned.1.call-update) | async-done | bytes 33554448 | tf_op jit(solution)/shard_map/all_gather | solution.py:65
  254.1 17.9 %convert_multiply_fusion.4 = (f32[256,2048]{1,0:T(8,128)}, f32[256,2048]{1,0:T(8,128)}) fusion(bf16[256,2048]{1,0:T(8,128)(2,1)} %param.16, bf16[256,8192]{1,0:T(8,128)(2,1)} %all-gather.9.cloned.1.call-done, bf16[8192,2048]{1,0:T(8,128)(2,1)} %all-gather.11.cloned.1.call-done), kind=kOutput, calls=%fused_computation.57 | convolution fusion | flops 8590983168 | bytes 42991616 | tf_op jit(solution)/shard_map/dot_general | solution.py:63
  274.3 343.8 %while.68 = (s32[]{:T(128)}, f32[16,2048]{1,0:T(8,128)}, f32[16,2048]{1,0:T(8,128)}, f32[4,64,2048]{2,1,0:T(8,128)}, f32[4,64,2048]{2,1,0:T(8,128)}, /*index=5*/...) while((s32[]{:T(128)}, f32[16,2048]{1,0:T(8,128)}, ...), condition=%wide.region_9.10_spmd.clone.clone.clone, body=%wide.region_6.0_spmd.clone.clone.clone.sunk | while | flops 1639882752 | bytes 212862208 | solution.py:81
  283.5 8.8 %fusion.55 = f32[32768,64]{0,1:T(8,128)S(1)} fusion(f32[64,32768]{1,0:T(8,128)S(1)} %bitcast.143), kind=kOutput, calls=%fused_computation.41.clone.1 | convolution fusion | flops 1610620928 | bytes 16777216 | tf_op jit(solution)/shard_map/while/body/eval_jaxpr/dot_general | solution.py:74
  300.3 10.9 %multiply_reduce_fusion.7 = (f32[64,2048]{1,0:T(8,128)S(1)}, f32[64,16,2048]{2,1,0:T(8,128)}, f32[64,16,2048]{2,1,0:T(8,128)S(1)}, f32[64,16,2048]{2,1,0:T(8,128)}) fusion(f32[16,2048]{1,0:T(8,128)} %copy-done.7, f32[16,2048]{1,0:T(8,128)} %get-tuple-element.1005, f32[64]{0:T(128)S(1)} %get-tuple-element.1028, f32[16,2048]{1,0:T(8,128)} %copy-done, ...), kind=kLoop, calls=%fused_computation.35.clone.1 | loop fusion | flops 14548992 | bytes 34603520 | tf_op jit(solution)/shard_map/while/body/eval_jaxpr/reduce_sum | solution.py:79
  317.1 11.7 %copy.32 = f32[8,8,16,2048]{3,1,2,0:T(8,128)} copy(f32[8,8,16,2048]{3,2,1,0:T(8,128)} %bitcast.148) | data formatting | bytes 16777216 | tf_op jit(solution)/shard_map/while
  328.7 11.7 %copy.33 = f32[8,8,16,2048]{3,1,2,0:T(8,128)} copy(f32[8,8,16,2048]{3,2,1,0:T(8,128)} %bitcast.145) | data formatting | bytes 16777216 | tf_op jit(solution)/shard_map/while
  348.6 9.5 %fusion.56 = f32[32768]{0:T(1024)S(1)} fusion(f32[64,32768]{1,0:T(8,128)} %bitcast.149, f32[64,32768]{1,0:T(8,128)} %bitcast.150, f32[32768,64]{0,1:T(8,128)S(1)} %fusion.55, f32[64,32768]{1,0:T(8,128)} %bitcast.151, f32[32768]{0:T(1024)S(1)} %bitcast.153), kind=kLoop, calls=%fused_computation.31.clone.1 | loop fusion | flops 10452992 | bytes 33816576 | tf_op jit(solution)/shard_map/while/body/eval_jaxpr/reduce_sum | solution.py:78
  368.4 9.0 %fusion.55 = f32[32768,64]{0,1:T(8,128)S(1)} fusion(f32[64,32768]{1,0:T(8,128)S(1)} %bitcast.143), kind=kOutput, calls=%fused_computation.41.clone.1 | convolution fusion | flops 1610620928 | bytes 16777216 | tf_op jit(solution)/shard_map/while/body/eval_jaxpr/dot_general | solution.py:74
  385.4 10.7 %multiply_reduce_fusion.7 = (f32[64,2048]{1,0:T(8,128)S(1)}, f32[64,16,2048]{2,1,0:T(8,128)}, f32[64,16,2048]{2,1,0:T(8,128)S(1)}, f32[64,16,2048]{2,1,0:T(8,128)}) fusion(f32[16,2048]{1,0:T(8,128)} %copy-done.7, f32[16,2048]{1,0:T(8,128)} %get-tuple-element.1005, f32[64]{0:T(128)S(1)} %get-tuple-element.1028, f32[16,2048]{1,0:T(8,128)} %copy-done, ...), kind=kLoop, calls=%fused_computation.35.clone.1 | loop fusion | flops 14548992 | bytes 34603520 | tf_op jit(solution)/shard_map/while/body/eval_jaxpr/reduce_sum | solution.py:79
  402.0 11.7 %copy.32 = f32[8,8,16,2048]{3,1,2,0:T(8,128)} copy(f32[8,8,16,2048]{3,2,1,0:T(8,128)} %bitcast.148) | data formatting | bytes 16777216 | tf_op jit(solution)/shard_map/while
  413.6 11.7 %copy.33 = f32[8,8,16,2048]{3,1,2,0:T(8,128)} copy(f32[8,8,16,2048]{3,2,1,0:T(8,128)} %bitcast.145) | data formatting | bytes 16777216 | tf_op jit(solution)/shard_map/while
  433.6 9.5 %fusion.56 = f32[32768]{0:T(1024)S(1)} fusion(f32[64,32768]{1,0:T(8,128)} %bitcast.149, f32[64,32768]{1,0:T(8,128)} %bitcast.150, f32[32768,64]{0,1:T(8,128)S(1)} %fusion.55, f32[64,32768]{1,0:T(8,128)} %bitcast.151, f32[32768]{0:T(1024)S(1)} %bitcast.153), kind=kLoop, calls=%fused_computation.31.clone.1 | loop fusion | flops 10452992 | bytes 33816576 | tf_op jit(solution)/shard_map/while/body/eval_jaxpr/reduce_sum | solution.py:78
  453.5 8.8 %fusion.55 = f32[32768,64]{0,1:T(8,128)S(1)} fusion(f32[64,32768]{1,0:T(8,128)S(1)} %bitcast.143), kind=kOutput, calls=%fused_computation.41.clone.1 | convolution fusion | flops 1610620928 | bytes 16777216 | tf_op jit(solution)/shard_map/while/body/eval_jaxpr/dot_general | solution.py:74
  470.2 10.7 %multiply_reduce_fusion.7 = (f32[64,2048]{1,0:T(8,128)S(1)}, f32[64,16,2048]{2,1,0:T(8,128)}, f32[64,16,2048]{2,1,0:T(8,128)S(1)}, f32[64,16,2048]{2,1,0:T(8,128)}) fusion(f32[16,2048]{1,0:T(8,128)} %copy-done.7, f32[16,2048]{1,0:T(8,128)} %get-tuple-element.1005, f32[64]{0:T(128)S(1)} %get-tuple-element.1028, f32[16,2048]{1,0:T(8,128)} %copy-done, ...), kind=kLoop, calls=%fused_computation.35.clone.1 | loop fusion | flops 14548992 | bytes 34603520 | tf_op jit(solution)/shard_map/while/body/eval_jaxpr/reduce_sum | solution.py:79
  486.8 11.7 %copy.32 = f32[8,8,16,2048]{3,1,2,0:T(8,128)} copy(f32[8,8,16,2048]{3,2,1,0:T(8,128)} %bitcast.148) | data formatting | bytes 16777216 | tf_op jit(solution)/shard_map/while
  498.5 11.7 %copy.33 = f32[8,8,16,2048]{3,1,2,0:T(8,128)} copy(f32[8,8,16,2048]{3,2,1,0:T(8,128)} %bitcast.145) | data formatting | bytes 16777216 | tf_op jit(solution)/shard_map/while
  518.6 9.5 %fusion.56 = f32[32768]{0:T(1024)S(1)} fusion(f32[64,32768]{1,0:T(8,128)} %bitcast.149, f32[64,32768]{1,0:T(8,128)} %bitcast.150, f32[32768,64]{0,1:T(8,128)S(1)} %fusion.55, f32[64,32768]{1,0:T(8,128)} %bitcast.151, f32[32768]{0:T(1024)S(1)} %bitcast.153), kind=kLoop, calls=%fused_computation.31.clone.1 | loop fusion | flops 10452992 | bytes 33816576 | tf_op jit(solution)/shard_map/while/body/eval_jaxpr/reduce_sum | solution.py:78
  538.3 8.8 %fusion.55 = f32[32768,64]{0,1:T(8,128)S(1)} fusion(f32[64,32768]{1,0:T(8,128)S(1)} %bitcast.143), kind=kOutput, calls=%fused_computation.41.clone.1 | convolution fusion | flops 1610620928 | bytes 16777216 | tf_op jit(solution)/shard_map/while/body/eval_jaxpr/dot_general | solution.py:74
  555.1 10.9 %multiply_reduce_fusion.7 = (f32[64,2048]{1,0:T(8,128)S(1)}, f32[64,16,2048]{2,1,0:T(8,128)}, f32[64,16,2048]{2,1,0:T(8,128)S(1)}, f32[64,16,2048]{2,1,0:T(8,128)}) fusion(f32[16,2048]{1,0:T(8,128)} %copy-done.7, f32[16,2048]{1,0:T(8,128)} %get-tuple-element.1005, f32[64]{0:T(128)S(1)} %get-tuple-element.1028, f32[16,2048]{1,0:T(8,128)} %copy-done, ...), kind=kLoop, calls=%fused_computation.35.clone.1 | loop fusion | flops 14548992 | bytes 34603520 | tf_op jit(solution)/shard_map/while/body/eval_jaxpr/reduce_sum | solution.py:79
  571.9 11.7 %copy.32 = f32[8,8,16,2048]{3,1,2,0:T(8,128)} copy(f32[8,8,16,2048]{3,2,1,0:T(8,128)} %bitcast.148) | data formatting | bytes 16777216 | tf_op jit(solution)/shard_map/while
  583.5 11.7 %copy.33 = f32[8,8,16,2048]{3,1,2,0:T(8,128)} copy(f32[8,8,16,2048]{3,2,1,0:T(8,128)} %bitcast.145) | data formatting | bytes 16777216 | tf_op jit(solution)/shard_map/while
  603.4 9.5 %fusion.56 = f32[32768]{0:T(1024)S(1)} fusion(f32[64,32768]{1,0:T(8,128)} %bitcast.149, f32[64,32768]{1,0:T(8,128)} %bitcast.150, f32[32768,64]{0,1:T(8,128)S(1)} %fusion.55, f32[64,32768]{1,0:T(8,128)} %bitcast.151, f32[32768]{0:T(1024)S(1)} %bitcast.153), kind=kLoop, calls=%fused_computation.31.clone.1 | loop fusion | flops 10452992 | bytes 33816576 | tf_op jit(solution)/shard_map/while/body/eval_jaxpr/reduce_sum | solution.py:78
  618.2 13.6 %while.65 = (s32[]{:T(128)}, f32[16,2048]{1,0:T(8,128)}, s32[]{:T(128)}, f32[8,16,2048]{2,1,0:T(8,128)}, f32[8,16,2048]{2,1,0:T(8,128)}, /*index=5*/s32[]{:T(128)}, s32[]{:T(128)}) while((s32[]{:T(128)}, f32[16,2048]{1,0:T(8,128)}, s32[]{:T(128)}, f32[8,16,2048]{2,1,0:T(8,128)}, f32[8,16,2048]{2,1,0:T(8,128)}, ...), condition=%wide.region_4.5_spmd.clone, body=%wide.region_3.4_spmd.clone.sunk | while | flops 131076 | bytes 524397 | solution.py:22
  631.8 9.8 %all-gather.17.cloned.1.call-done = f32[128,2048]{1,0:T(8,128)} async-done(((f32[16,2048]{1,0:T(8,128)}), f32[128,2048]{1,0:T(8,128)}) %all-gather.17.cloned.1.call-update) | async-done | bytes 1048592 | tf_op jit(solution)/shard_map/all_gather | solution.py:9
  641.6 13.5 %while.66 = (s32[]{:T(128)}, f32[16,2048]{1,0:T(8,128)}, s32[]{:T(128)}, f32[8,16,2048]{2,1,0:T(8,128)}, f32[8,16,2048]{2,1,0:T(8,128)}, /*index=5*/s32[]{:T(128)}, s32[]{:T(128)}, s32[]{:T(128)}, s32[]{:T(128)}) while((s32[]{:T(128)}, f32[16,2048]{1,0:T(8,128)}, s32[]{:T(128)}, f32[8,16,2048]{2,1,0:T(8,128)}, ...), condition=%wide.region_11.12_spmd.clone, body=%wide.region_10.11_spmd.clone.sunk | while | flops 131080 | bytes 524459 | solution.py:22
  657.1 21.9 %multiply_reduce_fusion.2 = (f32[256,2048]{1,0:T(8,128)S(1)}, f32[256,2048]{1,0:T(8,128)S(1)}) fusion(f32[16,2048]{1,0:T(8,128)S(1)} %get-tuple-element.781, f32[256]{0:T(256)S(1)} %copy-done.20, f32[16,2048]{1,0:T(8,128)S(1)} %get-tuple-element.1121, f32[16,2048]{1,0:T(8,128)S(1)} %get-tuple-element.782, f32[256]{0:T(256)} %convert_add_fusion), kind=kLoop, calls=%fused_computation.44 | loop fusion | flops 49283072 | bytes 4589568 | tf_op jit(solution)/shard_map/reduce_sum | solution.py:99
  682.1 28.6 %all-reduce.2.cloned.1.call-done = f32[16,2048]{1,0:T(8,128)} async-done(((f32[16,2048]{1,0:T(8,128)}), f32[16,2048]{1,0:T(8,128)}) %all-reduce.2.cloned.1.call-update) | async-done | bytes 131088 | tf_op jit(solution)/shard_map/psum | solution.py:108
  (229 shorter events, 248.1 us)
Async XLA Ops:
  7.2 110.4 %all-gather.9.cloned.1.call-start = ((), (), s32[]{:S(2)}) async-start(), calls=%async_computation | async-start | bytes 5242880 | tf_op jit(solution)/shard_map/all_gather | solution.py:62
  7.9 246.2 %all-gather.11.cloned.1.call-start = ((), (), s32[]{:S(2)}) async-start(), calls=%async_computation.1 | async-start | bytes 37748736 | tf_op jit(solution)/shard_map/all_gather | solution.py:65
  8.7 609.5 %all-gather.13.cloned.1.call-start = ((), (), s32[]{:S(2)}) async-start(), calls=%async_computation.3 | async-start | bytes 1179648 | tf_op jit(solution)/shard_map/all_gather | solution.py:9
  10.5 607.8 %all-gather.15.cloned.1.call-start = ((), (), s32[]{:S(2)}) async-start(), calls=%async_computation.4 | async-start | bytes 1179648 | tf_op jit(solution)/shard_map/all_gather | solution.py:9
  116.3 525.3 %all-gather.17.cloned.1.call-start = ((), (), s32[]{:S(2)}) async-start(), calls=%async_computation.5 | async-start | bytes 1179648 | tf_op jit(solution)/shard_map/all_gather | solution.py:9
  274.3 382.7 %copy-start.20 = (f32[256]{0:T(256)S(1)}, f32[256]{0:T(256)}, u32[]{:S(2)}) copy-start(f32[256]{0:T(256)} %convert_subtract_fusion) | copy-start | bytes 3076
  348.6 9.5 %copy-start.13 = (f32[16,2048]{1,0:T(8,128)S(1)}, f32[16,2048]{1,0:T(8,128)}, u32[]{:S(2)}) copy-start(f32[16,2048]{1,0:T(8,128)} %get-tuple-element.1006) | copy-start | bytes 393220 | tf_op jit(solution)/shard_map/while
  348.6 10.5 %copy-start.1 = (f32[16,2048]{1,0:T(8,128)S(1)}, f32[16,2048]{1,0:T(8,128)}, u32[]{:S(2)}) copy-start(f32[16,2048]{1,0:T(8,128)} %copy-done) | copy-start | bytes 393220 | tf_op jit(solution)/shard_map/while
  348.6 10.5 %copy-start.3 = (f32[4,64,2048]{2,1,0:T(8,128)S(1)}, f32[4,64,2048]{2,1,0:T(8,128)}, u32[]{:S(2)}) copy-start(f32[4,64,2048]{2,1,0:T(8,128)} %copy-done.2) | copy-start | bytes 6291460 | tf_op jit(solution)/shard_map/while
  348.6 10.5 %copy-start.6 = (f32[16,2048]{1,0:T(8,128)S(1)}, f32[16,2048]{1,0:T(8,128)}, u32[]{:S(2)}) copy-start(f32[16,2048]{1,0:T(8,128)} %copy-done.5) | copy-start | bytes 393220 | tf_op jit(solution)/shard_map/while
  348.6 10.5 %copy-start.8 = (f32[16,2048]{1,0:T(8,128)S(1)}, f32[16,2048]{1,0:T(8,128)}, u32[]{:S(2)}) copy-start(f32[16,2048]{1,0:T(8,128)} %copy-done.7) | copy-start | bytes 393220 | tf_op jit(solution)/shard_map/while
  433.5 9.5 %copy-start.13 = (f32[16,2048]{1,0:T(8,128)S(1)}, f32[16,2048]{1,0:T(8,128)}, u32[]{:S(2)}) copy-start(f32[16,2048]{1,0:T(8,128)} %get-tuple-element.1006) | copy-start | bytes 393220 | tf_op jit(solution)/shard_map/while
  433.5 10.5 %copy-start.1 = (f32[16,2048]{1,0:T(8,128)S(1)}, f32[16,2048]{1,0:T(8,128)}, u32[]{:S(2)}) copy-start(f32[16,2048]{1,0:T(8,128)} %copy-done) | copy-start | bytes 393220 | tf_op jit(solution)/shard_map/while
  433.5 10.5 %copy-start.3 = (f32[4,64,2048]{2,1,0:T(8,128)S(1)}, f32[4,64,2048]{2,1,0:T(8,128)}, u32[]{:S(2)}) copy-start(f32[4,64,2048]{2,1,0:T(8,128)} %copy-done.2) | copy-start | bytes 6291460 | tf_op jit(solution)/shard_map/while
  433.5 10.5 %copy-start.6 = (f32[16,2048]{1,0:T(8,128)S(1)}, f32[16,2048]{1,0:T(8,128)}, u32[]{:S(2)}) copy-start(f32[16,2048]{1,0:T(8,128)} %copy-done.5) | copy-start | bytes 393220 | tf_op jit(solution)/shard_map/while
  433.5 10.5 %copy-start.8 = (f32[16,2048]{1,0:T(8,128)S(1)}, f32[16,2048]{1,0:T(8,128)}, u32[]{:S(2)}) copy-start(f32[16,2048]{1,0:T(8,128)} %copy-done.7) | copy-start | bytes 393220 | tf_op jit(solution)/shard_map/while
  518.6 10.4 %copy-start.1 = (f32[16,2048]{1,0:T(8,128)S(1)}, f32[16,2048]{1,0:T(8,128)}, u32[]{:S(2)}) copy-start(f32[16,2048]{1,0:T(8,128)} %copy-done) | copy-start | bytes 393220 | tf_op jit(solution)/shard_map/while
  518.6 10.4 %copy-start.3 = (f32[4,64,2048]{2,1,0:T(8,128)S(1)}, f32[4,64,2048]{2,1,0:T(8,128)}, u32[]{:S(2)}) copy-start(f32[4,64,2048]{2,1,0:T(8,128)} %copy-done.2) | copy-start | bytes 6291460 | tf_op jit(solution)/shard_map/while
  518.6 10.4 %copy-start.6 = (f32[16,2048]{1,0:T(8,128)S(1)}, f32[16,2048]{1,0:T(8,128)}, u32[]{:S(2)}) copy-start(f32[16,2048]{1,0:T(8,128)} %copy-done.5) | copy-start | bytes 393220 | tf_op jit(solution)/shard_map/while
  518.6 10.4 %copy-start.8 = (f32[16,2048]{1,0:T(8,128)S(1)}, f32[16,2048]{1,0:T(8,128)}, u32[]{:S(2)}) copy-start(f32[16,2048]{1,0:T(8,128)} %copy-done.7) | copy-start | bytes 393220 | tf_op jit(solution)/shard_map/while
  603.4 9.5 %copy-start.13 = (f32[16,2048]{1,0:T(8,128)S(1)}, f32[16,2048]{1,0:T(8,128)}, u32[]{:S(2)}) copy-start(f32[16,2048]{1,0:T(8,128)} %get-tuple-element.1006) | copy-start | bytes 393220 | tf_op jit(solution)/shard_map/while
  603.4 10.5 %copy-start.1 = (f32[16,2048]{1,0:T(8,128)S(1)}, f32[16,2048]{1,0:T(8,128)}, u32[]{:S(2)}) copy-start(f32[16,2048]{1,0:T(8,128)} %copy-done) | copy-start | bytes 393220 | tf_op jit(solution)/shard_map/while
  603.4 10.5 %copy-start.3 = (f32[4,64,2048]{2,1,0:T(8,128)S(1)}, f32[4,64,2048]{2,1,0:T(8,128)}, u32[]{:S(2)}) copy-start(f32[4,64,2048]{2,1,0:T(8,128)} %copy-done.2) | copy-start | bytes 6291460 | tf_op jit(solution)/shard_map/while
  603.4 10.5 %copy-start.6 = (f32[16,2048]{1,0:T(8,128)S(1)}, f32[16,2048]{1,0:T(8,128)}, u32[]{:S(2)}) copy-start(f32[16,2048]{1,0:T(8,128)} %copy-done.5) | copy-start | bytes 393220 | tf_op jit(solution)/shard_map/while
  603.4 10.5 %copy-start.8 = (f32[16,2048]{1,0:T(8,128)S(1)}, f32[16,2048]{1,0:T(8,128)}, u32[]{:S(2)}) copy-start(f32[16,2048]{1,0:T(8,128)} %copy-done.7) | copy-start | bytes 393220 | tf_op jit(solution)/shard_map/while
  618.1 92.5 %all-reduce.2.cloned.1.call-start = ((), (), s32[]{:S(2)}) async-start(), calls=%async_computation.2 | async-start | bytes 262144 | tf_op jit(solution)/shard_map/psum | solution.py:108
  657.0 22.0 %copy-start.11 = (f32[4,64,2048]{2,1,0:T(8,128)S(1)}, f32[4,64,2048]{2,1,0:T(8,128)}, u32[]{:S(2)}) copy-start(f32[4,64,2048]{2,1,0:T(8,128)} %get-tuple-element.500) | copy-start | bytes 6291460
  657.0 22.0 %copy-start.12 = (f32[4,64,2048]{2,1,0:T(8,128)S(1)}, f32[4,64,2048]{2,1,0:T(8,128)}, u32[]{:S(2)}) copy-start(f32[4,64,2048]{2,1,0:T(8,128)} %get-tuple-element.497) | copy-start | bytes 6291460
  657.1 22.0 %copy-start.15 = (bf16[256,2048]{1,0:T(8,128)(2,1)S(1)}, bf16[256,2048]{1,0:T(8,128)(2,1)}, u32[]{:S(2)}) copy-start(bf16[256,2048]{1,0:T(8,128)(2,1)} %param.17) | copy-start | bytes 3145732
  657.1 22.0 %copy-start.16 = (bf16[256,2048]{1,0:T(8,128)(2,1)S(1)}, bf16[256,2048]{1,0:T(8,128)(2,1)}, u32[]{:S(2)}) copy-start(bf16[256,2048]{1,0:T(8,128)(2,1)} %param.18) | copy-start | bytes 3145732
  657.1 22.0 %copy-start.17 = (f32[256,2048]{1,0:T(8,128)S(1)}, f32[256,2048]{1,0:T(8,128)}, u32[]{:S(2)}) copy-start(f32[256,2048]{1,0:T(8,128)} %get-tuple-element.788) | copy-start | bytes 6291460
  657.1 22.0 %copy-start.19 = (f32[256]{0:T(256)S(1)}, f32[256]{0:T(256)}, u32[]{:S(2)}) copy-start(f32[256]{0:T(256)} %copy-done.18) | copy-start | bytes 3076
  (28 other events, 124.1 us)
Sparse Core Ops, SparseCore 0:
  9.6 83.4 all-gather.8
  94.9 159.1 all-gather.10
  256.6 23.3 all-gather.12
  282.3 23.3 all-gather.14
  618.2 23.3 all-gather.16
  657.1 53.4 all-reduce.1
where the time goes:
time: 721 us; the launch traced here: 719 us
  local copies, waits for them, and re-layouts  266 us (37%)
  waiting for transfers between devices  176 us (24%)
  other arithmetic  169 us (23%)
  matrix products  87.4 us (12%)
  between operations  14.7 us (2%)
    while x120, local copies, waits for them, and re-layouts  225 us
    all_gather x1, waiting for transfers between devices, body(): lax.all_gather(out_weight, 'ctx', axis=0, tiled=True)  137 us
    reduce_sum x4, other arithmetic, backward_block(): return ((states[0], running), jnp.sum(filter_gain[None] * states, axis=1))  43.2 us
    reduce_sum x4, other arithmetic, backward_block(): running = running + jnp.sum(input_blk[:, None, :] * states, axis=0)  37.9 us
    dot_general x4, matrix products, backward_block(): jnp.dot(upper_ones, scaled, precision=lax.Precision.HIGHEST)  35.5 us
    dot_general x4, matrix products, forward_block(): jnp.dot(lower_ones, scaled, precision=lax.Precision.HIGHEST)  34 us
    psum x1, waiting for transfers between devices, body(): filter_grad = lax.psum(filter_terms, 'ctx')  28.6 us
    select_n x16, other arithmetic, turn(): return jax.tree.map(lambda a, b: jnp.where(reached, a, b), new, before)  27.1 us
  transfers between devices with their start and end apart: 6, of which 3 were waited for; matrix products, arithmetic and copies ran while one was open for 70% of the time, Pallas kernels for 0%

commit v1 on v0

v1 whole, which is shorter than its diff:
```python
import functools

import jax
import jax.numpy as jnp
from jax import lax
from jax.experimental import pallas as pl
from jax.experimental.pallas import tpu as pltpu
from jax.sharding import PartitionSpec as P


def carried_in(shard, axis, combine, identity, reverse):
    devices, here = (lax.axis_size(axis), lax.axis_index(axis))
    everything = jax.tree.map(lambda part: lax.all_gather(part, axis), shard)
    start = jax.tree.map(
        lambda part, zero: jnp.broadcast_to(jnp.asarray(zero, part.dtype), part.shape),
        shard,
        identity,
    )

    def turn(k, before):
        at = devices - 1 - k if reverse else k
        reached = at > here if reverse else at < here
        new = combine(before, jax.tree.map(lambda part: part[at], everything))
        return jax.tree.map(lambda a, b: jnp.where(reached, a, b), new, before)

    return lax.fori_loop(0, devices, turn, start)


def chain_join(earlier, later):
    return (earlier[0] * later[0], later[0] * earlier[1] + later[1])


ROWS = 64
TILE = 512


def scan_kernel(x_ref, g_ref, a_ref, gain_ref, fin_ref, bin_ref, conv_ref, igrad_ref, run_ref):
    tokens = x_ref.shape[0]
    blocks = tokens // ROWS
    modes = a_ref.shape[0]
    row = lax.broadcasted_iota(jnp.int32, (ROWS, ROWS), 0)
    col = lax.broadcasted_iota(jnp.int32, (ROWS, ROWS), 1)
    lower = (row >= col).astype(jnp.float32)
    upper = (row <= col).astype(jnp.float32)
    places = lax.broadcasted_iota(jnp.int32, (ROWS, 1), 0).astype(jnp.float32)
    conv_ref[...] = jnp.zeros_like(conv_ref)
    igrad_ref[...] = jnp.zeros_like(igrad_ref)

    def mode(m, _):
        a = a_ref[pl.ds(m, 1), :]
        gain = gain_ref[pl.ds(m, 1), :]
        rising = jnp.exp(a * places)
        falling = jnp.exp(-a * places)
        step = jnp.exp(-a)
        tail = jnp.exp(-a * float(ROWS))
        carried = fin_ref[pl.ds(m, 1), :]
        for b in range(blocks):
            xb = x_ref[pl.ds(b * ROWS, ROWS), :]
            summed = jnp.dot(lower, rising * xb, precision=lax.Precision.HIGHEST,
                             preferred_element_type=jnp.float32)
            states = falling * (summed + step * carried)
            conv_ref[pl.ds(b * ROWS, ROWS), :] += gain * states
            carried = states[ROWS - 1:ROWS, :]
        carried = bin_ref[pl.ds(m, 1), :]
        running = jnp.zeros_like(a)
        for b in reversed(range(blocks)):
            gb = g_ref[pl.ds(b * ROWS, ROWS), :]
            xb = x_ref[pl.ds(b * ROWS, ROWS), :]
            summed = jnp.dot(upper, falling * gb, precision=lax.Precision.HIGHEST,
                             preferred_element_type=jnp.float32)
            states = rising * (summed + tail * carried)
            running = running + jnp.sum(xb * states, axis=0, keepdims=True)
            igrad_ref[pl.ds(b * ROWS, ROWS), :] += gain * states
            carried = states[0:1, :]
        run_ref[pl.ds(m, 1), :] = running
        return 0

    lax.fori_loop(0, modes, mode, 0)


def local_scans(inputs, conv_grad, decay_rate, filter_gain, forward_in, backward_in):
    tokens, chans = inputs.shape
    modes = decay_rate.shape[0]
    tile = min(TILE, chans)
    seq = pl.BlockSpec((tokens, tile), lambda j: (0, j))
    par = pl.BlockSpec((modes, tile), lambda j: (0, j))
    return pl.pallas_call(
        scan_kernel,
        grid=(chans // tile,),
        in_specs=[seq, seq, par, par, par, par],
        out_specs=[seq, seq, par],
        out_shape=[
            jax.ShapeDtypeStruct((tokens, chans), jnp.float32),
            jax.ShapeDtypeStruct((tokens, chans), jnp.float32),
            jax.ShapeDtypeStruct((modes, chans), jnp.float32),
        ],
        compiler_params=pltpu.CompilerParams(dimension_semantics=("parallel",)),
    )(inputs, conv_grad, decay_rate, filter_gain, forward_in, backward_in)


def body(query_act, key_act, value_act, out_grad, out_weight, token_mask, decay_rate, residue):
    tokens_here = query_act.shape[0]
    live = token_mask.astype(jnp.float32)[:, None]
    inputs = live * key_act.astype(jnp.float32) * value_act.astype(jnp.float32)
    root_gain = jnp.sqrt(-jnp.expm1(-2.0 * decay_rate))
    filter_gain = residue * root_gain
    full_grad = lax.all_gather(out_grad, "ch", axis=1, tiled=True)
    gate_grad = jnp.dot(
        full_grad,
        lax.all_gather(out_weight, "ctx", axis=0, tiled=True),
        preferred_element_type=jnp.float32,
    )
    conv_grad = gate_grad * query_act.astype(jnp.float32)
    token_places = jnp.arange(tokens_here).astype(jnp.float32)[:, None, None]
    end_state = jnp.sum(
        jnp.exp(-decay_rate[None] * (tokens_here - 1.0 - token_places)) * inputs[:, None, :], axis=0
    )
    start_state = jnp.sum(
        jnp.exp(-decay_rate[None] * token_places) * conv_grad[:, None, :], axis=0
    )
    span_decay = jnp.exp(-decay_rate * tokens_here)
    zeros = jnp.zeros_like(decay_rate)
    forward_in = carried_in(
        (span_decay, end_state), "ctx", chain_join, (jnp.ones_like(span_decay), zeros), False
    )[1]
    backward_in = carried_in(
        (span_decay, start_state), "ctx", chain_join, (jnp.ones_like(span_decay), zeros), True
    )[1]
    conv, input_grad, running = local_scans(
        inputs, conv_grad, decay_rate, filter_gain, forward_in, backward_in
    )
    query_grad = (gate_grad * conv).astype(jnp.bfloat16)
    key_grad = (live * input_grad * value_act.astype(jnp.float32)).astype(jnp.bfloat16)
    value_grad = (live * input_grad * key_act.astype(jnp.float32)).astype(jnp.bfloat16)
    filter_grad = lax.psum(root_gain * running, "ctx")
    return (query_grad, key_grad, value_grad, filter_grad)


def solution(mesh):
    placed = (
        P("ctx", "ch"),
        P("ctx", "ch"),
        P("ctx", "ch"),
        P("ctx", "ch"),
        P("ctx", "ch"),
        P("ctx"),
        P(None, "ch"),
        P(None, "ch"),
    )
    return jax.shard_map(
        body,
        mesh=mesh,
        in_specs=placed,
        out_specs=(P("ctx", "ch"), P("ctx", "ch"), P("ctx", "ch"), P(None, "ch")),
        check_vma=False,
    )
```

time: 721 us -> 477 us (0.66)
  local copies, waits for them, and re-layouts: 266 us -> 1.74 us
  waiting for transfers between devices: 176 us -> 333 us
  other arithmetic: 169 us -> 39.6 us
  matrix products: 87.4 us -> 17.6 us
  Pallas kernels: 0 us -> 69.7 us
    while x120 -> x0, local copies, waits for them, and re-layouts: 225 us -> none
    reduce_sum x13 -> x1, other arithmetic: 120 us -> 13.1 us  [body(): jnp.sum(jnp.exp(-decay_rate[None] * token_places) * conv_grad[:, None, :]...]
    all_gather x1, waiting for transfers between devices: 0.01 us -> 81.7 us  [body(): full_grad = lax.all_gather(out_grad, 'ch', axis=1, tiled=True)]
    pallas_call x0 -> x1, Pallas kernels: none -> 69.7 us  [local_scans(): pl.pallas_call(scan_kernel, grid=(chans // tile,), in_specs=[seq, seq, pa...]
    dot_general x8 -> x0, matrix products: 69.5 us -> none  [the longest x4 35.5 us: backward_block(): jnp.dot(upper_ones, scaled, precision=lax.Precision.HIGHEST)]
    all_gather x3, waiting for transfers between devices: 9.87 us -> 39.8 us  [carried_in(): everything = jax.tree.map(lambda part: lax.all_gather(part, axis), shard)]
    all_gather x1, waiting for transfers between devices: 137 us -> 161 us  [body(): lax.all_gather(out_weight, 'ctx', axis=0, tiled=True)]
    mul x12 -> x0, local copies, waits for them, and re-layouts: 21.9 us -> none  [the longest x8 21.7 us: backward_block(): running = running + jnp.sum(input_blk[:, None, :] * states, axis=0)]
  transfers between devices with their start and end apart: 6 -> 6, of which waited for: 3 -> 5; matrix products, arithmetic and copies ran while one was open for 70% -> 10% of each run, Pallas kernels for 0% -> 0%
where the time goes in v1:
time: 477 us; the launch traced here: 476 us
  waiting for transfers between devices  333 us (70%)
  Pallas kernels  69.7 us (15%)
  other arithmetic  39.6 us (8%)
  matrix products  17.6 us (4%)
  between operations  14.3 us (3%)
    all_gather x1, waiting for transfers between devices, body(): lax.all_gather(out_weight, 'ctx', axis=0, tiled=True)  161 us
    all_gather x1, waiting for transfers between devices, body(): full_grad = lax.all_gather(out_grad, 'ch', axis=1, tiled=True)  81.7 us
    pallas_call x1, Pallas kernels, local_scans(): pl.pallas_call(scan_kernel, grid=(chans // tile,), in_specs=[seq, seq, pa...  69.7 us
    psum x1, waiting for transfers between devices, body(): filter_grad = lax.psum(root_gain * running, 'ctx')  48.3 us
    all_gather x3, waiting for transfers between devices, carried_in(): everything = jax.tree.map(lambda part: lax.all_gather(part, axis), shard)  39.8 us
    dot_general x1, matrix products, body(): jnp.dot(full_grad, lax.all_gather(out_weight, 'ctx', axis=0, tiled=True),...  17.6 us
    select_n x16, other arithmetic, turn(): return jax.tree.map(lambda a, b: jnp.where(reached, a, b), new, before)  17.1 us
    reduce_sum x1, other arithmetic, body(): jnp.sum(jnp.exp(-decay_rate[None] * token_places) * conv_grad[:, None, :]...  13.1 us
  transfers between devices with their start and end apart: 6, of which 5 were waited for; matrix products, arithmetic and copies ran while one was open for 10% of the time, Pallas kernels for 0%

profile of v1, /device:TPU:0, one launch (start us, length us, event | category | flops | bytes accessed | tf_op | source)
XLA Modules:
  0.0 476.2 jit_solution(7261510699154061344)
XLA Ops:
  8.0 0.7 all-gather.11.cloned.1.call-update
  8.9 0.8 fusion.6
  9.8 1.6 convert_multiply_fusion.1.x_ref
  11.4 81.7 %all-gather.9.cloned.1.call-done = bf16[256,8192]{1,0:T(8,128)(2,1)} async-done(((bf16[256,2048]{1,0:T(8,128)(2,1)}), bf16[256,8192]{1,0:T(8,128)(2,1)}) %all-gather.9.cloned.1.call-update) | async-done | bytes 4194320 | tf_op jit(solution)/shard_map/all_gather | solution.py:107
  93.0 161.1 %all-gather.11.cloned.1.call-done = bf16[8192,2048]{1,0:T(8,128)(2,1)} async-done(((bf16[1024,2048]{1,0:T(8,128)(2,1)}), bf16[8192,2048]{1,0:T(8,128)(2,1)}) %all-gather.11.cloned.1.call-update) | async-done | bytes 33554448 | tf_op jit(solution)/shard_map/all_gather | solution.py:110
  254.1 17.6 %convert_multiply_fusion.4 = (f32[256,2048]{1,0:T(8,128)S(1)}, f32[256,2048]{1,0:T(8,128)}) fusion(bf16[256,2048]{1,0:T(8,128)(2,1)} %param.12, bf16[256,8192]{1,0:T(8,128)(2,1)} %all-gather.9.cloned.1.call-done, bf16[8192,2048]{1,0:T(8,128)(2,1)} %all-gather.11.cloned.1.call-done), kind=kOutput, calls=%fused_computation.15 | convolution fusion | flops 8590983168 | bytes 42991616 | tf_op jit(solution)/shard_map/dot_general | solution.py:108
  271.7 13.1 %multiply_reduce_fusion = (f32[16,2048]{1,0:T(8,128)}, f32[16,2048]{1,0:T(8,128)}) fusion(f32[256,2048]{1,0:T(8,128)S(1)} %get-tuple-element.301.g_ref, f32[256]{0:T(256)S(1)} %iota_convert_fusion, f32[16,2048]{1,0:T(8,128)S(1)} %get-tuple-element.298, f32[256,2048]{1,0:T(8,128)S(1)} %convert_multiply_fusion.1.x_ref, f32[256]{0:T(256)S(1)} %broadcast_subtract_fusion), kind=kLoop, calls=%fused_computation.6 | loop fusion | flops 50266112 | bytes 4589568 | tf_op jit(solution)/shard_map/reduce_sum | solution.py:118
  285.5 22.9 %all-gather.17.cloned.1.call-done = f32[128,2048]{1,0:T(8,128)} async-done(((f32[16,2048]{1,0:T(8,128)}), f32[128,2048]{1,0:T(8,128)}) %all-gather.17.cloned.1.call-update) | async-done | bytes 1048592 | tf_op jit(solution)/shard_map/all_gather | solution.py:13
  308.4 8.8 %while.31 = (s32[]{:T(128)}, f32[16,2048]{1,0:T(8,128)S(1)}, s32[]{:T(128)}, f32[8,16,2048]{2,1,0:T(8,128)}, f32[8,16,2048]{2,1,0:T(8,128)}, /*index=5*/s32[]{:T(128)}, s32[]{:T(128)}, s32[]{:T(128)}, s32[]{:T(128)}) while((s32[]{:T(128)}, f32[16,2048]{1,0:T(8,128)S(1)}, s32[]{:T(128)}, f32[8,16,2048]{2,1,0:T(8,128)}, ...), condition=%wide.region_5.6_spmd.clone, body=%wide.region_4.5_spmd.clone.sunk | while | flops 131080 | bytes 524451 | solution.py:26
  308.4 1.1 fusion.12
  309.5 1.1 fusion.12
  310.6 1.1 fusion.12
  311.7 1.1 fusion.12
  312.8 1.1 fusion.12
  313.9 1.1 fusion.12
  315.0 1.1 fusion.12
  316.1 1.1 fusion.12
  317.2 16.9 %all-gather.15.cloned.1.call-done = f32[128,2048]{1,0:T(8,128)} async-done(((f32[16,2048]{1,0:T(8,128)}), f32[128,2048]{1,0:T(8,128)}) %all-gather.15.cloned.1.call-update) | async-done | bytes 1048592 | tf_op jit(solution)/shard_map/all_gather | solution.py:13
  334.1 8.7 %while.30 = (s32[]{:T(128)}, f32[16,2048]{1,0:T(8,128)S(1)}, s32[]{:T(128)}, f32[8,16,2048]{2,1,0:T(8,128)}, f32[8,16,2048]{2,1,0:T(8,128)}, /*index=5*/s32[]{:T(128)}, s32[]{:T(128)}) while((s32[]{:T(128)}, f32[16,2048]{1,0:T(8,128)S(1)}, s32[]{:T(128)}, f32[8,16,2048]{2,1,0:T(8,128)}, f32[8,16,2048]{2,1,0:T(8,128)}, ...), condition=%wide.region_2.3_spmd.clone, body=%wide.region_1.0_spmd.clone.sunk | while | flops 131076 | bytes 524389 | solution.py:26
  334.1 1.1 fusion.11
  335.2 1.1 fusion.11
  336.3 1.1 fusion.11
  337.4 1.1 fusion.11
  338.5 1.1 fusion.11
  339.6 1.1 fusion.11
  340.6 1.1 fusion.11
  341.7 1.1 fusion.11
  342.8 69.7 %shard_map.111 = (f32[256,2048]{1,0:T(8,128)}, f32[256,2048]{1,0:T(8,128)}, f32[16,2048]{1,0:T(8,128)}) custom-call(f32[256,2048]{1,0:T(8,128)} %copy-done, f32[256,2048]{1,0:T(8,128)} %copy-done.3, f32[16,2048]{1,0:T(8,128)} %a_ref.1, f32[16,2048]{1,0:T(8,128)} %get-tuple-element.300.gain_ref, f32[16,2048]{1,0:T(8,128)S(1)} %get-tuple-element.233.fin_ref, ...), custom_call_target="tpu_custom_call" | custom-call | tf_op jit(solution)/shard_map/pallas_call | solution.py:87
  412.6 1.7 fusion.4
  414.2 5.3 %fusion.2 = (bf16[256,2048]{1,0:T(8,128)(2,1)}, bf16[256,2048]{1,0:T(8,128)(2,1)}, bf16[256,2048]{1,0:T(8,128)(2,1)}) fusion(bf16[256,2048]{1,0:T(8,128)(2,1)S(1)} %copy-done.1, f32[256,2048]{1,0:T(8,128)} %get-tuple-element.236, f32[256]{0:T(256)S(1)} %convert_element_type.35, bf16[256,2048]{1,0:T(8,128)(2,1)S(1)} %copy-done.2, ...), kind=kLoop, calls=%fused_computation.12 | loop fusion | flops 4718592 | bytes 11535360 | tf_op jit(solution)/shard_map/convert_element_type | solution.py:134
  419.5 48.3 %all-reduce.2.cloned.1.call-done = f32[16,2048]{1,0:T(8,128)} async-done(((f32[16,2048]{1,0:T(8,128)}), f32[16,2048]{1,0:T(8,128)}) %all-reduce.2.cloned.1.call-update) | async-done | bytes 131088 | tf_op jit(solution)/shard_map/psum | solution.py:135
  467.8 1.6 copy.25
  (33 shorter events, 1.7 us)
Async XLA Ops:
  7.2 85.9 %all-gather.9.cloned.1.call-start = ((), (), s32[]{:S(2)}) async-start(), calls=%async_computation | async-start | bytes 5242880 | tf_op jit(solution)/shard_map/all_gather | solution.py:107
  7.9 0.9 copy-start.4
  7.9 1.0 copy-start.6
  7.9 1.8 copy-start.7
  7.9 1.9 copy-start.1
  7.9 246.2 %all-gather.11.cloned.1.call-start = ((), (), s32[]{:S(2)}) async-start(), calls=%async_computation.1 | async-start | bytes 37748736 | tf_op jit(solution)/shard_map/all_gather | solution.py:110
  8.7 276.8 %all-gather.13.cloned.1.call-start = ((), (), s32[]{:S(2)}) async-start(), calls=%async_computation.3 | async-start | bytes 1179648 | tf_op jit(solution)/shard_map/all_gather | solution.py:13
  9.7 298.7 %all-gather.17.cloned.1.call-start = ((), (), s32[]{:S(2)}) async-start(), calls=%async_computation.5 | async-start | bytes 1179648 | tf_op jit(solution)/shard_map/all_gather | solution.py:13
  11.4 260.4 %copy-start = (f32[256,2048]{1,0:T(8,128)}, f32[256,2048]{1,0:T(8,128)S(1)}, u32[]{:S(2)}) copy-start(f32[256,2048]{1,0:T(8,128)S(1)} %convert_multiply_fusion.1.x_ref) | copy-start | bytes 6291460
  271.7 13.1 %copy-start.3 = (f32[256,2048]{1,0:T(8,128)}, f32[256,2048]{1,0:T(8,128)S(1)}, u32[]{:S(2)}) copy-start(f32[256,2048]{1,0:T(8,128)S(1)} %get-tuple-element.301.g_ref) | copy-start | bytes 6291460
  284.9 49.2 %all-gather.15.cloned.1.call-start = ((), (), s32[]{:S(2)}) async-start(), calls=%async_computation.4 | async-start | bytes 1179648 | tf_op jit(solution)/shard_map/all_gather | solution.py:13
  285.5 182.4 %all-reduce.2.cloned.1.call-start = ((), (), s32[]{:S(2)}) async-start(), calls=%async_computation.2 | async-start | bytes 262144 | tf_op jit(solution)/shard_map/psum | solution.py:135
  342.8 69.7 %copy-start.5 = (f32[16,2048]{1,0:T(8,128)S(1)}, f32[16,2048]{1,0:T(8,128)}, u32[]{:S(2)}) copy-start(f32[16,2048]{1,0:T(8,128)} %a_ref.1) | copy-start | bytes 393220
  342.8 71.4 %copy-start.2 = (bf16[256,2048]{1,0:T(8,128)(2,1)S(1)}, bf16[256,2048]{1,0:T(8,128)(2,1)}, u32[]{:S(2)}) copy-start(bf16[256,2048]{1,0:T(8,128)(2,1)} %param.14) | copy-start | bytes 3145732
Sparse Core Ops, SparseCore 0:
  9.5 83.4 all-gather.8
  94.9 159.1 all-gather.10
  256.6 23.3 all-gather.12
  285.0 23.3 all-gather.16
  310.7 23.3 all-gather.14
  414.4 53.4 all-reduce.1

commit v2 on v1

--- a/solution.py
+++ b/solution.py
@@ -1,33 +1,9 @@
-import functools
-
 import jax
 import jax.numpy as jnp
 from jax import lax
 from jax.experimental import pallas as pl
 from jax.experimental.pallas import tpu as pltpu
 from jax.sharding import PartitionSpec as P
-
-
-def carried_in(shard, axis, combine, identity, reverse):
-    devices, here = (lax.axis_size(axis), lax.axis_index(axis))
-    everything = jax.tree.map(lambda part: lax.all_gather(part, axis), shard)
-    start = jax.tree.map(
-        lambda part, zero: jnp.broadcast_to(jnp.asarray(zero, part.dtype), part.shape),
-        shard,
-        identity,
-    )
-
-    def turn(k, before):
-        at = devices - 1 - k if reverse else k
-        reached = at > here if reverse else at < here
-        new = combine(before, jax.tree.map(lambda part: part[at], everything))
-        return jax.tree.map(lambda a, b: jnp.where(reached, a, b), new, before)
-
-    return lax.fori_loop(0, devices, turn, start)
-
-
-def chain_join(earlier, later):
-    return (earlier[0] * later[0], later[0] * earlier[1] + later[1])
 
 
 ROWS = 64
@@ -119,13 +95,16 @@
         jnp.exp(-decay_rate[None] * token_places) * conv_grad[:, None, :], axis=0
     )
     span_decay = jnp.exp(-decay_rate * tokens_here)
-    zeros = jnp.zeros_like(decay_rate)
-    forward_in = carried_in(
-        (span_decay, end_state), "ctx", chain_join, (jnp.ones_like(span_decay), zeros), False
-    )[1]
-    backward_in = carried_in(
-        (span_decay, start_state), "ctx", chain_join, (jnp.ones_like(span_decay), zeros), True
-    )[1]
+    everything = lax.all_gather(jnp.stack([span_decay, end_state, start_state]), "ctx")
+    devices, here = (lax.axis_size("ctx"), lax.axis_index("ctx"))
+    forward_in = jnp.zeros_like(decay_rate)
+    for k in range(devices):
+        joined = everything[k, 0] * forward_in + everything[k, 1]
+        forward_in = jnp.where(k < here, joined, forward_in)
+    backward_in = jnp.zeros_like(decay_rate)
+    for k in reversed(range(devices)):
+        joined = everything[k, 0] * backward_in + everything[k, 2]
+        backward_in = jnp.where(k > here, joined, backward_in)
     conv, input_grad, running = local_scans(
         inputs, conv_grad, decay_rate, filter_gain, forward_in, backward_in
     )

time: 477 us -> 455 us (0.954)
  other arithmetic: 39.6 us -> 27.3 us
  waiting for transfers between devices: 333 us -> 325 us
    select_n x16 -> x2, other arithmetic: 17.1 us -> 4.75 us  [the longest x1 2.37 us: body(): forward_in = jnp.where(k < here, joined, forward_in)]
    all_gather x3 -> x1, waiting for transfers between devices: 39.8 us -> 32.3 us  [body(): lax.all_gather(jnp.stack([span_decay, end_state, start_state]), 'ctx')]
  transfers between devices with their start and end apart: 6 -> 4, of which waited for: 5 -> 4; matrix products, arithmetic and copies ran while one was open for 10% -> 2% of each run, Pallas kernels for 0% -> 0%
where the time goes in v2:
time: 455 us
  waiting for transfers between devices  325 us (71%)
  Pallas kernels  69.7 us (15%)
  other arithmetic  27.3 us (6%)
  matrix products  17.5 us (4%)
  between operations  13.9 us (3%)
    all_gather x1, waiting for transfers between devices, body(): lax.all_gather(out_weight, 'ctx', axis=0, tiled=True)  161 us
    all_gather x1, waiting for transfers between devices, body(): full_grad = lax.all_gather(out_grad, 'ch', axis=1, tiled=True)  81.8 us
    pallas_call x1, Pallas kernels, local_scans(): pl.pallas_call(scan_kernel, grid=(chans // tile,), in_specs=[seq, seq, pa...  69.7 us
    psum x1, waiting for transfers between devices, body(): filter_grad = lax.psum(root_gain * running, 'ctx')  48.3 us
    all_gather x1, waiting for transfers between devices, body(): lax.all_gather(jnp.stack([span_decay, end_state, start_state]), 'ctx')  32.3 us
    dot_general x1, matrix products, body(): jnp.dot(full_grad, lax.all_gather(out_weight, 'ctx', axis=0, tiled=True),...  17.5 us
    reduce_sum x1, other arithmetic, body(): jnp.sum(jnp.exp(-decay_rate[None] * (tokens_here - 1.0 - token_places)) *...  12.5 us
  transfers between devices with their start and end apart: 4, of which 4 were waited for; matrix products, arithmetic and copies ran while one was open for 2% of the time, Pallas kernels for 0%

profile of v2, /device:TPU:0, one launch (start us, length us, event | category | flops | bytes accessed | tf_op | source)
XLA Modules:
  0.0 455.1 jit_solution(4360385450536637142)
XLA Ops:
  7.2 0.0 all-gather.5.cloned.1.call-start
  7.2 0.7 all-gather.5.cloned.1.call-update
  7.9 0.0 copy-start.7
  7.9 0.0 copy-start.4
  7.9 0.0 copy-start.6
  7.9 0.0 copy-start.1
  7.9 0.0 all-gather.7.cloned.1.call-start
  8.0 0.7 all-gather.7.cloned.1.call-update
  8.7 0.0 all-gather.9.cloned.1.call-start
  8.7 0.0 copy-done.7
  8.8 0.0 copy-done.4
  8.8 0.1 copy-done.6
  8.9 0.8 exponential_bitcast_fusion
  9.6 1.6 convert_multiply_fusion.1.x_ref
  11.2 0.0 copy-start
  11.2 81.8 %all-gather.5.cloned.1.call-done = bf16[256,8192]{1,0:T(8,128)(2,1)} async-done(((bf16[256,2048]{1,0:T(8,128)(2,1)}), bf16[256,8192]{1,0:T(8,128)(2,1)}) %all-gather.5.cloned.1.call-update) | async-done | bytes 4194320 | tf_op jit(solution)/shard_map/all_gather | solution.py:83
  93.0 161.1 %all-gather.7.cloned.1.call-done = bf16[8192,2048]{1,0:T(8,128)(2,1)} async-done(((bf16[1024,2048]{1,0:T(8,128)(2,1)}), bf16[8192,2048]{1,0:T(8,128)(2,1)}) %all-gather.7.cloned.1.call-update) | async-done | bytes 33554448 | tf_op jit(solution)/shard_map/all_gather | solution.py:86
  254.1 17.5 %convert_multiply_fusion.4 = (f32[256,2048]{1,0:T(8,128)S(1)}, f32[256,2048]{1,0:T(8,128)}) fusion(bf16[256,2048]{1,0:T(8,128)(2,1)} %param.8, bf16[256,8192]{1,0:T(8,128)(2,1)} %all-gather.5.cloned.1.call-done, bf16[8192,2048]{1,0:T(8,128)(2,1)} %all-gather.7.cloned.1.call-done), kind=kOutput, calls=%fused_computation.9 | convolution fusion | flops 8590983168 | bytes 42991616 | tf_op jit(solution)/shard_map/dot_general | solution.py:84
  271.7 12.5 %multiply_reduce_fusion.1 = (f32[16,2048]{1,0:T(8,128)S(1)}, f32[16,2048]{1,0:T(8,128)S(1)}) fusion(f32[256,2048]{1,0:T(8,128)S(1)} %convert_multiply_fusion.1.x_ref, f32[256]{0:T(256)S(1)} %broadcast_subtract_fusion, f32[16,2048]{1,0:T(8,128)S(1)} %get-tuple-element.16, f32[256,2048]{1,0:T(8,128)S(1)} %get-tuple-element.17.g_ref, f32[256]{0:T(256)S(1)} %iota_convert_fusion), kind=kLoop, calls=%fused_computation.1 | loop fusion | flops 50266112 | bytes 4589568 | tf_op jit(solution)/shard_map/reduce_sum | solution.py:91
  284.2 0.8 pad_maximum_fusion
  284.9 0.0 all-gather.9.cloned.1.call-update
  285.0 0.0 all-reduce.2.cloned.1.call-start
  285.0 32.3 %all-gather.9.cloned.1.call-done = f32[24,16,2048]{2,1,0:T(8,128)} async-done(((f32[3,16,2048]{2,1,0:T(8,128)}), f32[24,16,2048]{2,1,0:T(8,128)}) %all-gather.9.cloned.1.call-update) | async-done | bytes 3145744 | tf_op jit(solution)/shard_map/all_gather | solution.py:98
  317.3 2.4 fusion.3.bin_ref
  319.7 2.4 fusion.19.fin_ref
  322.0 69.7 %shard_map.111 = (f32[256,2048]{1,0:T(8,128)}, f32[256,2048]{1,0:T(8,128)}, f32[16,2048]{1,0:T(8,128)}) custom-call(f32[256,2048]{1,0:T(8,128)} %copy-done, f32[256,2048]{1,0:T(8,128)} %copy-done.3, f32[16,2048]{1,0:T(8,128)} %a_ref.1, f32[16,2048]{1,0:T(8,128)} %get-tuple-element.15.gain_ref, f32[16,2048]{1,0:T(8,128)} %fusion.19.fin_ref, ...), custom_call_target="tpu_custom_call" | custom-call | tf_op jit(solution)/shard_map/pallas_call | solution.py:63
  391.7 0.0 copy-done.5
  391.7 1.6 fusion.34
  393.4 0.0 all-reduce.2.cloned.1.call-update
  393.4 5.3 %fusion = (bf16[256,2048]{1,0:T(8,128)(2,1)}, bf16[256,2048]{1,0:T(8,128)(2,1)}, bf16[256,2048]{1,0:T(8,128)(2,1)}) fusion(bf16[256,2048]{1,0:T(8,128)(2,1)S(1)} %copy-done.1, f32[256,2048]{1,0:T(8,128)} %get-tuple-element.8, f32[256]{0:T(256)S(1)} %convert_element_type.35, bf16[256,2048]{1,0:T(8,128)(2,1)S(1)} %copy-done.2, ...), kind=kLoop, calls=%fused_computation.6 | loop fusion | flops 4718592 | bytes 11535360 | tf_op jit(solution)/shard_map/convert_element_type | solution.py:113
  398.7 48.3 %all-reduce.2.cloned.1.call-done = f32[16,2048]{1,0:T(8,128)} async-done(((f32[16,2048]{1,0:T(8,128)}), f32[16,2048]{1,0:T(8,128)}) %all-reduce.2.cloned.1.call-update) | async-done | bytes 131088 | tf_op jit(solution)/shard_map/psum | solution.py:114
  447.0 1.6 copy.13
  (10 shorter events, 0.0 us)
Async XLA Ops:
  7.2 85.9 %all-gather.5.cloned.1.call-start = ((), (), s32[]{:S(2)}) async-start(), calls=%async_computation | async-start | bytes 5242880 | tf_op jit(solution)/shard_map/all_gather | solution.py:83
  7.9 0.8 copy-start.7
  7.9 0.9 copy-start.4
  7.9 1.0 copy-start.6
  7.9 1.7 copy-start.1
  7.9 246.2 %all-gather.7.cloned.1.call-start = ((), (), s32[]{:S(2)}) async-start(), calls=%async_computation.1 | async-start | bytes 37748736 | tf_op jit(solution)/shard_map/all_gather | solution.py:86
  8.7 308.6 %all-gather.9.cloned.1.call-start = ((), (), s32[]{:S(2)}) async-start(), calls=%async_computation.3 | async-start | bytes 3538944 | tf_op jit(solution)/shard_map/all_gather | solution.py:98
  11.2 260.4 %copy-start = (f32[256,2048]{1,0:T(8,128)}, f32[256,2048]{1,0:T(8,128)S(1)}, u32[]{:S(2)}) copy-start(f32[256,2048]{1,0:T(8,128)S(1)} %convert_multiply_fusion.1.x_ref) | copy-start | bytes 6291460
  271.6 12.5 %copy-start.3 = (f32[256,2048]{1,0:T(8,128)}, f32[256,2048]{1,0:T(8,128)S(1)}, u32[]{:S(2)}) copy-start(f32[256,2048]{1,0:T(8,128)S(1)} %get-tuple-element.17.g_ref) | copy-start | bytes 6291460
  285.0 162.0 %all-reduce.2.cloned.1.call-start = ((), (), s32[]{:S(2)}) async-start(), calls=%async_computation.2 | async-start | bytes 262144 | tf_op jit(solution)/shard_map/psum | solution.py:114
  322.0 69.7 %copy-start.5 = (f32[16,2048]{1,0:T(8,128)S(1)}, f32[16,2048]{1,0:T(8,128)}, u32[]{:S(2)}) copy-start(f32[16,2048]{1,0:T(8,128)} %a_ref.1) | copy-start | bytes 393220
  322.0 71.4 %copy-start.2 = (bf16[256,2048]{1,0:T(8,128)(2,1)S(1)}, bf16[256,2048]{1,0:T(8,128)(2,1)}, u32[]{:S(2)}) copy-start(bf16[256,2048]{1,0:T(8,128)(2,1)} %param.10) | copy-start | bytes 3145732
Sparse Core Ops, SparseCore 0:
  9.5 83.4 all-gather.4
  94.9 159.1 all-gather.6
  285.1 32.1 all-gather.8
  393.5 53.4 all-reduce.1

commit v3 on v2

--- a/solution.py
+++ b/solution.py
@@ -111,7 +111,7 @@
     query_grad = (gate_grad * conv).astype(jnp.bfloat16)
     key_grad = (live * input_grad * value_act.astype(jnp.float32)).astype(jnp.bfloat16)
     value_grad = (live * input_grad * key_act.astype(jnp.float32)).astype(jnp.bfloat16)
-    filter_grad = lax.psum(root_gain * running, "ctx")
+    filter_grad = jnp.sum(lax.all_gather(root_gain * running, "ctx"), axis=0)
     return (query_grad, key_grad, value_grad, filter_grad)
 
 

time: 455 us -> 426 us (0.936)
  waiting for transfers between devices: 325 us -> 295 us
    psum x1 -> x0, waiting for transfers between devices: 48.3 us -> none  [body(): filter_grad = lax.psum(root_gain * running, 'ctx')]
    all_gather x0 -> x1, waiting for transfers between devices: none -> 18.2 us  [body(): filter_grad = jnp.sum(lax.all_gather(root_gain * running, 'ctx'), axis=0)]
where the time goes in v3:
time: 426 us; the launch traced here: 425 us
  waiting for transfers between devices  295 us (69%)
  Pallas kernels  69.7 us (16%)
  other arithmetic  29.2 us (7%)
  matrix products  17.5 us (4%)
  between operations  13.9 us (3%)
    all_gather x1, waiting for transfers between devices, body(): lax.all_gather(out_weight, 'ctx', axis=0, tiled=True)  161 us
    all_gather x1, waiting for transfers between devices, body(): full_grad = lax.all_gather(out_grad, 'ch', axis=1, tiled=True)  81.8 us
    pallas_call x1, Pallas kernels, local_scans(): pl.pallas_call(scan_kernel, grid=(chans // tile,), in_specs=[seq, seq, pa...  69.7 us
    all_gather x1, waiting for transfers between devices, body(): lax.all_gather(jnp.stack([span_decay, end_state, start_state]), 'ctx')  32.3 us
    all_gather x1, waiting for transfers between devices, body(): filter_grad = jnp.sum(lax.all_gather(root_gain * running, 'ctx'), axis=0)  18.2 us
    dot_general x1, matrix products, body(): jnp.dot(full_grad, lax.all_gather(out_weight, 'ctx', axis=0, tiled=True),...  17.5 us
    reduce_sum x1, other arithmetic, body(): jnp.sum(jnp.exp(-decay_rate[None] * (tokens_here - 1.0 - token_places)) *...  12.5 us
  transfers between devices with their start and end apart: 4, of which 4 were waited for; matrix products, arithmetic and copies ran while one was open for 2% of the time, Pallas kernels for 0%

profile of v3, /device:TPU:0, one launch (start us, length us, event | category | flops | bytes accessed | tf_op | source)
XLA Modules:
  0.0 425.4 jit_solution(6142931432378888494)
XLA Ops:
  7.2 0.0 all-gather.7.cloned.1.call-start
  7.2 0.7 all-gather.7.cloned.1.call-update
  7.9 0.0 copy-start.7
  7.9 0.0 copy-start.4
  7.9 0.0 copy-start.6
  7.9 0.0 copy-start.1
  7.9 0.0 all-gather.9.cloned.1.call-start
  8.0 0.7 all-gather.9.cloned.1.call-update
  8.7 0.0 all-gather.11.cloned.1.call-start
  8.7 0.0 copy-done.7
  8.8 0.0 copy-done.4
  8.8 0.1 copy-done.6
  8.9 0.8 exponential_bitcast_fusion
  9.6 1.6 convert_multiply_fusion.1.x_ref
  11.2 0.0 copy-start
  11.2 81.8 %all-gather.7.cloned.1.call-done = bf16[256,8192]{1,0:T(8,128)(2,1)} async-done(((bf16[256,2048]{1,0:T(8,128)(2,1)}), bf16[256,8192]{1,0:T(8,128)(2,1)}) %all-gather.7.cloned.1.call-update) | async-done | bytes 4194320 | tf_op jit(solution)/shard_map/all_gather | solution.py:83
  93.0 161.1 %all-gather.9.cloned.1.call-done = bf16[8192,2048]{1,0:T(8,128)(2,1)} async-done(((bf16[1024,2048]{1,0:T(8,128)(2,1)}), bf16[8192,2048]{1,0:T(8,128)(2,1)}) %all-gather.9.cloned.1.call-update) | async-done | bytes 33554448 | tf_op jit(solution)/shard_map/all_gather | solution.py:86
  254.1 17.5 %convert_multiply_fusion.4 = (f32[256,2048]{1,0:T(8,128)S(1)}, f32[256,2048]{1,0:T(8,128)}) fusion(bf16[256,2048]{1,0:T(8,128)(2,1)} %param.8, bf16[256,8192]{1,0:T(8,128)(2,1)} %all-gather.7.cloned.1.call-done, bf16[8192,2048]{1,0:T(8,128)(2,1)} %all-gather.9.cloned.1.call-done), kind=kOutput, calls=%fused_computation.9 | convolution fusion | flops 8590983168 | bytes 42991616 | tf_op jit(solution)/shard_map/dot_general | solution.py:84
  271.7 12.5 %multiply_reduce_fusion.1 = (f32[16,2048]{1,0:T(8,128)S(1)}, f32[16,2048]{1,0:T(8,128)S(1)}) fusion(f32[256,2048]{1,0:T(8,128)S(1)} %convert_multiply_fusion.1.x_ref, f32[256]{0:T(256)S(1)} %broadcast_subtract_fusion, f32[16,2048]{1,0:T(8,128)S(1)} %get-tuple-element.16, f32[256,2048]{1,0:T(8,128)S(1)} %get-tuple-element.17.g_ref, f32[256]{0:T(256)S(1)} %iota_convert_fusion), kind=kLoop, calls=%fused_computation.1 | loop fusion | flops 50266112 | bytes 4589568 | tf_op jit(solution)/shard_map/reduce_sum | solution.py:91
  284.2 0.8 pad_maximum_fusion
  284.9 0.0 all-gather.11.cloned.1.call-update
  285.0 0.0 all-gather.13.cloned.1.call-start
  285.0 32.3 %all-gather.11.cloned.1.call-done = f32[24,16,2048]{2,1,0:T(8,128)} async-done(((f32[3,16,2048]{2,1,0:T(8,128)}), f32[24,16,2048]{2,1,0:T(8,128)}) %all-gather.11.cloned.1.call-update) | async-done | bytes 3145744 | tf_op jit(solution)/shard_map/all_gather | solution.py:98
  317.3 2.4 fusion.3.bin_ref
  319.7 2.4 fusion.19.fin_ref
  322.0 69.7 %shard_map.111 = (f32[256,2048]{1,0:T(8,128)}, f32[256,2048]{1,0:T(8,128)}, f32[16,2048]{1,0:T(8,128)}) custom-call(f32[256,2048]{1,0:T(8,128)} %copy-done, f32[256,2048]{1,0:T(8,128)} %copy-done.3, f32[16,2048]{1,0:T(8,128)} %a_ref.1, f32[16,2048]{1,0:T(8,128)} %get-tuple-element.15.gain_ref, f32[16,2048]{1,0:T(8,128)} %fusion.19.fin_ref, ...), custom_call_target="tpu_custom_call" | custom-call | tf_op jit(solution)/shard_map/pallas_call | solution.py:63
  391.7 0.0 copy-done.5
  391.7 1.6 fusion.34
  393.4 0.0 all-gather.13.cloned.1.call-update
  393.4 5.3 %fusion = (bf16[256,2048]{1,0:T(8,128)(2,1)}, bf16[256,2048]{1,0:T(8,128)(2,1)}, bf16[256,2048]{1,0:T(8,128)(2,1)}) fusion(bf16[256,2048]{1,0:T(8,128)(2,1)S(1)} %copy-done.1, f32[256,2048]{1,0:T(8,128)} %get-tuple-element.8, f32[256]{0:T(256)S(1)} %convert_element_type.35, bf16[256,2048]{1,0:T(8,128)(2,1)S(1)} %copy-done.2, ...), kind=kLoop, calls=%fused_computation.6 | loop fusion | flops 4718592 | bytes 11535360 | tf_op jit(solution)/shard_map/convert_element_type | solution.py:113
  398.7 18.2 %all-gather.13.cloned.1.call-done = f32[128,2048]{1,0:T(8,128)} async-done(((f32[16,2048]{1,0:T(8,128)}), f32[128,2048]{1,0:T(8,128)}) %all-gather.13.cloned.1.call-update) | async-done | bytes 1048592 | tf_op jit(solution)/shard_map/all_gather | solution.py:114
  416.9 1.9 reduce_sum.29
  (10 shorter events, 0.0 us)
Async XLA Ops:
  7.2 85.9 %all-gather.7.cloned.1.call-start = ((), (), s32[]{:S(2)}) async-start(), calls=%async_computation | async-start | bytes 5242880 | tf_op jit(solution)/shard_map/all_gather | solution.py:83
  7.9 0.8 copy-start.7
  7.9 0.9 copy-start.4
  7.9 1.0 copy-start.6
  7.9 1.7 copy-start.1
  7.9 246.2 %all-gather.9.cloned.1.call-start = ((), (), s32[]{:S(2)}) async-start(), calls=%async_computation.1 | async-start | bytes 37748736 | tf_op jit(solution)/shard_map/all_gather | solution.py:86
  8.7 308.6 %all-gather.11.cloned.1.call-start = ((), (), s32[]{:S(2)}) async-start(), calls=%async_computation.2 | async-start | bytes 3538944 | tf_op jit(solution)/shard_map/all_gather | solution.py:98
  11.2 260.4 %copy-start = (f32[256,2048]{1,0:T(8,128)}, f32[256,2048]{1,0:T(8,128)S(1)}, u32[]{:S(2)}) copy-start(f32[256,2048]{1,0:T(8,128)S(1)} %convert_multiply_fusion.1.x_ref) | copy-start | bytes 6291460
  271.6 12.5 %copy-start.3 = (f32[256,2048]{1,0:T(8,128)}, f32[256,2048]{1,0:T(8,128)S(1)}, u32[]{:S(2)}) copy-start(f32[256,2048]{1,0:T(8,128)S(1)} %get-tuple-element.17.g_ref) | copy-start | bytes 6291460
  285.0 132.0 %all-gather.13.cloned.1.call-start = ((), (), s32[]{:S(2)}) async-start(), calls=%async_computation.3 | async-start | bytes 1179648 | tf_op jit(solution)/shard_map/all_gather | solution.py:114
  322.0 69.7 %copy-start.5 = (f32[16,2048]{1,0:T(8,128)S(1)}, f32[16,2048]{1,0:T(8,128)}, u32[]{:S(2)}) copy-start(f32[16,2048]{1,0:T(8,128)} %a_ref.1) | copy-start | bytes 393220
  322.0 71.4 %copy-start.2 = (bf16[256,2048]{1,0:T(8,128)(2,1)S(1)}, bf16[256,2048]{1,0:T(8,128)(2,1)}, u32[]{:S(2)}) copy-start(bf16[256,2048]{1,0:T(8,128)(2,1)} %param.10) | copy-start | bytes 3145732
Sparse Core Ops, SparseCore 0:
  9.5 83.4 all-gather.6
  94.9 159.1 all-gather.8
  285.1 32.1 all-gather.10
  393.5 23.3 all-gather.12
